TPU v7x, 32 devices: a whole 2x2x4 slice. The times are simulated.
32 devices in a mesh: segment: 2 (over y), frame: 16 (over z, x, core).
Axes of the slice: x: 2, y: 2, z: 4, core: 2. Of those that a mesh axis runs over, the one named last changes fastest.
Arguments:
- noisy_clips: bfloat16 [4, 16, 16, 16, 512], P(None, 'frame'), may hold values from -6 to 6
- conv_first: bfloat16 [2, 9, 512, 512], P('segment', None, 'frame'), may hold values from -0.09375 to 0.09375
- conv_second: bfloat16 [2, 9, 512, 512], P('segment', None, 'frame'), may hold values from -0.09375 to 0.09375
- temporal: bfloat16 [2, 3, 512, 512], P('segment', None, 'frame'), may hold values from -0.15625 to 0.15625
Outputs:
- denoised: bfloat16 [4, 16, 16, 16, 512], P(None, 'frame', 'segment')
All inputs are finite; a program needn't handle non-finite values.
Results may differ from a plain program's by a relative error of at most 0.013.
Values may be sent and summed in bfloat16 or wider, within the bound.
A program may use at most 64 MiB of HBM per device.

v0:
```python
import jax
import jax.numpy as jnp
from jax import lax
from jax.sharding import PartitionSpec as P

skip_scale = 0.7071067811865476


def passed_along(shard, axis, by):
    length = lax.axis_size(axis)
    pairs = [(i, i + by) for i in range(length) if 0 <= i + by < length]
    return lax.ppermute(shard, axis, pairs)


def extended_2(cells, sides, width):
    for axis, dim in sides:
        count = lax.axis_size(axis)
        ends = count - 1
        head = lax.slice_in_dim(cells, 0, width, axis=dim)
        tail = lax.slice_in_dim(cells, cells.shape[dim] - width, cells.shape[dim], axis=dim)
        cells = jnp.concatenate(
            [
                lax.ppermute(tail, axis, [(i, (i + 1) % count) for i in range(ends)]),
                cells,
                lax.ppermute(head, axis, [((i + 1) % count, i) for i in range(ends)]),
            ],
            axis=dim,
        )
    return cells


def broadcast(shard, axis, root):
    mine = lax.axis_index(axis) == root
    return lax.psum(jnp.where(mine, shard, jnp.zeros_like(shard)), axis)


def spatial(field_in, kernel):
    extent = field_in.shape[1]
    channels = field_in.shape[3]
    padded = jnp.pad(field_in, ((0, 0), (1, 1), (1, 1), (0, 0)))
    accumulated = jnp.zeros((field_in.shape[0] * extent * extent, channels), jnp.float32)
    for row_shift in range(3):
        for col_shift in range(3):
            window = padded[
                :, row_shift : row_shift + extent, col_shift : col_shift + extent, :
            ].reshape(-1, channels)
            accumulated = accumulated + jnp.dot(
                window, kernel[3 * row_shift + col_shift], preferred_element_type=jnp.float32
            )
    return accumulated.reshape(field_in.shape)


def temporal_mix(extended, kernel, frame_local):
    channels = extended.shape[3]
    out_shape = (frame_local,) + extended.shape[1:]
    accumulated = jnp.zeros(out_shape, jnp.float32)
    for offset in range(3):
        window = extended[offset : offset + frame_local].reshape(-1, channels)
        accumulated = accumulated + jnp.dot(
            window, kernel[offset], preferred_element_type=jnp.float32
        ).reshape(out_shape)
    return accumulated


def on_device(noisy_clips, conv_first, conv_second, temporal):
    sections = lax.axis_size("segment")
    segment_id = lax.axis_index("segment")
    first_full, second_full, time_full = (
        lax.all_gather(conv_first, "frame", axis=2, tiled=True),
        lax.all_gather(conv_second, "frame", axis=2, tiled=True),
        lax.all_gather(temporal, "frame", axis=2, tiled=True),
    )
    first_kernel = first_full[0]
    second_kernel = second_full[0]
    time_kernel = time_full[0]
    clip_count = noisy_clips.shape[0]
    frame_local = noisy_clips.shape[1]
    side_len = noisy_clips.shape[2]
    block_shape = noisy_clips.shape[1:]
    tick_count = clip_count + sections - 1
    half_sections = sections // 2
    is_up = segment_id >= half_sections
    store_depth = max(half_sections - 1, 1)
    side_store = jnp.zeros((store_depth,) + block_shape, jnp.bfloat16)
    out_store = jnp.zeros(noisy_clips.shape, jnp.bfloat16)
    prev_out = jnp.zeros(block_shape, jnp.bfloat16)

    def tick_step(carry, tick_index):
        prev_out, side_store, out_store = carry
        clip_now = tick_index - segment_id
        active = (clip_now >= 0) & (clip_now < clip_count)
        clip_slot = jnp.clip(clip_now, 0, clip_count - 1)
        own_input = lax.dynamic_index_in_dim(noisy_clips, clip_slot, 0, keepdims=False)
        received, side_store = passed_along((prev_out, side_store), "segment", 1)
        entering = jnp.where(segment_id == 0, own_input, received)
        written = (jnp.arange(store_depth) == segment_id - 1) & (segment_id < half_sections)
        side_store = jnp.where(written[:, None, None, None, None], entering[None], side_store)
        stack_slot = jnp.clip(sections - 2 - segment_id, 0, store_depth - 1)
        stored = lax.dynamic_index_in_dim(side_store, stack_slot, 0, keepdims=False)
        skip_feature = jnp.where(segment_id == sections - 1, own_input, stored)
        joined = (
            (entering.astype(jnp.float32) + skip_feature.astype(jnp.float32)) * skip_scale
        ).astype(jnp.bfloat16)
        section_in = jnp.where(is_up, joined, entering)
        activated = lax.cond(
            active,
            lambda: jax.nn.silu(spatial(section_in, first_kernel)).astype(jnp.bfloat16),
            lambda: jnp.zeros(block_shape, jnp.bfloat16),
        )
        extended = extended_2(activated, (("frame", 0),), 1)

        def second_pass():
            branch_sum = spatial(activated, second_kernel) + temporal_mix(
                extended, time_kernel, frame_local
            )
            return (section_in.astype(jnp.float32) + jax.nn.silu(branch_sum)).astype(jnp.bfloat16)

        section_out = lax.cond(active, second_pass, lambda: jnp.zeros(block_shape, jnp.bfloat16))
        finished = (jnp.arange(clip_count) == clip_slot) & active & (segment_id == sections - 1)
        out_store = jnp.where(finished[:, None, None, None, None], section_out[None], out_store)
        return ((section_out, side_store, out_store), None)

    final_carry, unused = lax.scan(
        tick_step, (prev_out, side_store, out_store), jnp.arange(tick_count, dtype=jnp.int32)
    )
    delivered = broadcast(final_carry[2], "segment", sections - 1)
    slab_rows = side_len // sections
    return lax.dynamic_slice_in_dim(delivered, segment_id * slab_rows, slab_rows, 2)


def solution(mesh):
    in_specs = (
        P(None, "frame", None, None, None),
        P("segment", None, "frame", None),
        P("segment", None, "frame", None),
        P("segment", None, "frame", None),
    )
    out_specs = P(None, "frame", "segment", None, None)
    return jax.shard_map(
        on_device, mesh=mesh, in_specs=in_specs, out_specs=out_specs, check_vma=False
    )
```

profile of v0, /device:TPU:0, one launch (start us, length us, event | category | flops | bytes accessed | tf_op | source)
XLA Modules:
  0.0 428.6 jit_solution(14071804297938684224)
XLA Ops:
  8.8 43.1 %all-gather.8.cloned.1.call-done = bf16[1,3,512,512]{3,2,1,0:T(8,128)(2,1)} async-done(((bf16[1,3,32,512]{3,2,1,0:T(8,128)(2,1)}), bf16[1,3,512,512]{3,2,1,0:T(8,128)(2,1)}) %all-gather.8.cloned.1.call-update) | async-done | bytes 1572880 | tf_op jit(solution)/shard_map/all_gather | solution.py:71
  51.9 53.9 %all-gather.4.cloned.1.call-done = bf16[1,9,512,512]{3,2,1,0:T(8,128)(2,1)} async-done(((bf16[1,9,32,512]{3,2,1,0:T(8,128)(2,1)}), bf16[1,9,512,512]{3,2,1,0:T(8,128)(2,1)}) %all-gather.4.cloned.1.call-update) | async-done | bytes 4718608 | tf_op jit(solution)/shard_map/all_gather | solution.py:69
  105.8 53.7 %all-gather.6.cloned.1.call-done = bf16[1,9,512,512]{3,2,1,0:T(8,128)(2,1)} async-done(((bf16[1,9,32,512]{3,2,1,0:T(8,128)(2,1)}), bf16[1,9,512,512]{3,2,1,0:T(8,128)(2,1)}) %all-gather.6.cloned.1.call-update) | async-done | bytes 4718608 | tf_op jit(solution)/shard_map/all_gather | solution.py:70
  160.3 192.8 %while.17 = (s32[]{:T(128)}, bf16[1,16,16,512]{3,2,1,0:T(8,128)(2,1)}, bf16[1,1,16,16,512]{4,3,2,1,0:T(8,128)(2,1)}, bf16[4,1,16,16,512]{4,3,2,1,0:T(8,128)(2,1)...) while((s32[]{:T(128)}, ...), condition=%wide.region_5.6_spmd.clone, body=%wide.region_0.5_spmd.clone.sunk | while | flops 2824994816 | bytes 95421016 | solution.py:123
  160.3 3.4 collective-permute-start.1
  166.4 4.0 collective-permute-done.1
  170.3 5.0 %collective-permute-done = bf16[1,16,16,512]{3,2,1,0:T(8,128)(2,1)S(1)} collective-permute-done((bf16[1,16,16,512]{3,2,1,0:T(8,128)(2,1)}, bf16[1,16,16,512]{3,2,1,0:T(8,128)(2,1)S(1)}, u32[]{:S(2)}, u32[]{:S(2)}) %collective-permute-start) | collective-permute-done | bytes 262176 | tf_op jit(solution)/shard_map/while/body/eval_jaxpr/ppermute | solution.py:12
  175.3 2.0 fusion.72
  177.3 5.4 %conditional.6 = (bf16[1,16,16,512]{3,2,1,0:T(8,128)(2,1)S(1)}) conditional(s32[]{:T(128)} %convert_element_type.72, () %tuple.67, (bf16[1,16,16,512]{3,2,1,0:T(8,128)(2,1)S(1)}, bf16[9,512,512]{2,1,0:T(8,128)(2,1)}) %tuple.68), branch_computations={%region_1.1_spmd, %region_2.2_spmd} | conditional | flops 1209663488 | bytes 38010916 | solution.py:105
  177.6 1.5 fusion.8
  185.4 3.0 collective-permute-done.3
  188.4 8.0 %conditional.7 = (bf16[1,16,16,512]{3,2,1,0:T(8,128)(2,1)}) conditional(s32[]{:T(128)} %convert_element_type.72, () %tuple.66, (bf16[1,16,16,512]{3,2,1,0:T(8,128)(2,1)S(1)}, bf16[1,16,16,512]{3,2,1,0:T(8,128)(2,1)S(1)}, bf16[9,512,512]{2,1,0:T(8,128)(2,1)}, bf16[1,16,16,512]{3,2,1,0:T(8,128)(2,1)S(1)}, bf16[3,512,512]{2,1,0:T(8,128)(2,1)S(1)}, ...), branch_computations={%region_3.3_spmd, %region_4.4_spmd} | conditional | flops 1612972032 | bytes 42729508 | solution.py:118
  194.3 2.1 fusion.20
  203.8 4.5 %collective-permute-done = bf16[1,16,16,512]{3,2,1,0:T(8,128)(2,1)S(1)} collective-permute-done((bf16[1,16,16,512]{3,2,1,0:T(8,128)(2,1)}, bf16[1,16,16,512]{3,2,1,0:T(8,128)(2,1)S(1)}, u32[]{:S(2)}, u32[]{:S(2)}) %collective-permute-start) | collective-permute-done | bytes 262176 | tf_op jit(solution)/shard_map/while/body/eval_jaxpr/ppermute | solution.py:12
  208.3 2.0 fusion.72
  210.3 5.4 %conditional.6 = (bf16[1,16,16,512]{3,2,1,0:T(8,128)(2,1)S(1)}) conditional(s32[]{:T(128)} %convert_element_type.72, () %tuple.67, (bf16[1,16,16,512]{3,2,1,0:T(8,128)(2,1)S(1)}, bf16[9,512,512]{2,1,0:T(8,128)(2,1)}) %tuple.68), branch_computations={%region_1.1_spmd, %region_2.2_spmd} | conditional | flops 1209663488 | bytes 38010916 | solution.py:105
  210.6 1.5 fusion.8
  215.7 6.1 %collective-permute-start.2 = (bf16[1,16,16,512]{3,2,1,0:T(8,128)(2,1)S(1)}, bf16[1,16,16,512]{3,2,1,0:T(8,128)(2,1)S(1)}, u32[]{:S(2)}, u32[]{:S(2)}) collective-permute-start(bf16[1,16,16,512]{3,2,1,0:T(8,128)(2,1)S(1)} %get-tuple-element.419), channel_id=1, source_target_pairs={{0,1},{1,2},{2,3},{3,4},{4,5},{5,6},{6,7},{7,8},{8,9},{9,10},{10,1... | collective-permute-start | bytes 786440 | tf_op jit(solution)/shard_map/while/body/eval_jaxpr/ppermute | solution.py:23
  223.1 3.1 collective-permute-done.3
  226.2 8.0 %conditional.7 = (bf16[1,16,16,512]{3,2,1,0:T(8,128)(2,1)}) conditional(s32[]{:T(128)} %convert_element_type.72, () %tuple.66, (bf16[1,16,16,512]{3,2,1,0:T(8,128)(2,1)S(1)}, bf16[1,16,16,512]{3,2,1,0:T(8,128)(2,1)S(1)}, bf16[9,512,512]{2,1,0:T(8,128)(2,1)}, bf16[1,16,16,512]{3,2,1,0:T(8,128)(2,1)S(1)}, bf16[3,512,512]{2,1,0:T(8,128)(2,1)S(1)}, ...), branch_computations={%region_3.3_spmd, %region_4.4_spmd} | conditional | flops 1612972032 | bytes 42729508 | solution.py:118
  226.5 1.5 fusion.33
  232.1 2.1 fusion.20
  236.5 4.3 %collective-permute-start.1 = (bf16[1,1,16,16,512]{4,3,2,1,0:T(8,128)(2,1)S(1)}, bf16[1,1,16,16,512]{4,3,2,1,0:T(8,128)(2,1)S(1)}, u32[]{:S(2)}, u32[]{:S(2)}) collective-permute-start(bf16[1,1,16,16,512]{4,3,2,1,0:T(8,128)(2,1)S(1)} %broadcast_select_fusion.3), channel_id=1, source_target_pairs={{0,16},{1,17},{2,18},{3,19},{4,20},{5,21},{6,22},{7,23},{8,24},{9,... | collective-permute-start | bytes 786440 | tf_op jit(solution)/shard_map/while/body/eval_jaxpr/ppermute | solution.py:12
  244.7 3.7 collective-permute-done
  248.3 2.0 fusion.72
  250.3 5.4 %conditional.6 = (bf16[1,16,16,512]{3,2,1,0:T(8,128)(2,1)S(1)}) conditional(s32[]{:T(128)} %convert_element_type.72, () %tuple.67, (bf16[1,16,16,512]{3,2,1,0:T(8,128)(2,1)S(1)}, bf16[9,512,512]{2,1,0:T(8,128)(2,1)}) %tuple.68), branch_computations={%region_1.1_spmd, %region_2.2_spmd} | conditional | flops 1209663488 | bytes 38010916 | solution.py:105
  255.7 6.9 %collective-permute-start.2 = (bf16[1,16,16,512]{3,2,1,0:T(8,128)(2,1)S(1)}, bf16[1,16,16,512]{3,2,1,0:T(8,128)(2,1)S(1)}, u32[]{:S(2)}, u32[]{:S(2)}) collective-permute-start(bf16[1,16,16,512]{3,2,1,0:T(8,128)(2,1)S(1)} %get-tuple-element.419), channel_id=1, source_target_pairs={{0,1},{1,2},{2,3},{3,4},{4,5},{5,6},{6,7},{7,8},{8,9},{9,10},{10,1... | collective-permute-start | bytes 786440 | tf_op jit(solution)/shard_map/while/body/eval_jaxpr/ppermute | solution.py:23
  263.9 3.1 collective-permute-done.3
  267.0 8.0 %conditional.7 = (bf16[1,16,16,512]{3,2,1,0:T(8,128)(2,1)}) conditional(s32[]{:T(128)} %convert_element_type.72, () %tuple.66, (bf16[1,16,16,512]{3,2,1,0:T(8,128)(2,1)S(1)}, bf16[1,16,16,512]{3,2,1,0:T(8,128)(2,1)S(1)}, bf16[9,512,512]{2,1,0:T(8,128)(2,1)}, bf16[1,16,16,512]{3,2,1,0:T(8,128)(2,1)S(1)}, bf16[3,512,512]{2,1,0:T(8,128)(2,1)S(1)}, ...), branch_computations={%region_3.3_spmd, %region_4.4_spmd} | conditional | flops 1612972032 | bytes 42729508 | solution.py:118
  267.3 1.5 fusion.33
  272.9 2.1 fusion.20
  277.3 4.3 %collective-permute-start.1 = (bf16[1,1,16,16,512]{4,3,2,1,0:T(8,128)(2,1)S(1)}, bf16[1,1,16,16,512]{4,3,2,1,0:T(8,128)(2,1)S(1)}, u32[]{:S(2)}, u32[]{:S(2)}) collective-permute-start(bf16[1,1,16,16,512]{4,3,2,1,0:T(8,128)(2,1)S(1)} %broadcast_select_fusion.3), channel_id=1, source_target_pairs={{0,16},{1,17},{2,18},{3,19},{4,20},{5,21},{6,22},{7,23},{8,24},{9,... | collective-permute-start | bytes 786440 | tf_op jit(solution)/shard_map/while/body/eval_jaxpr/ppermute | solution.py:12
  285.5 2.9 collective-permute-done
  288.4 2.0 fusion.72
  290.3 5.4 %conditional.6 = (bf16[1,16,16,512]{3,2,1,0:T(8,128)(2,1)S(1)}) conditional(s32[]{:T(128)} %convert_element_type.72, () %tuple.67, (bf16[1,16,16,512]{3,2,1,0:T(8,128)(2,1)S(1)}, bf16[9,512,512]{2,1,0:T(8,128)(2,1)}) %tuple.68), branch_computations={%region_1.1_spmd, %region_2.2_spmd} | conditional | flops 1209663488 | bytes 38010916 | solution.py:105
  290.6 1.5 fusion.8
  295.8 8.5 %collective-permute-start.2 = (bf16[1,16,16,512]{3,2,1,0:T(8,128)(2,1)S(1)}, bf16[1,16,16,512]{3,2,1,0:T(8,128)(2,1)S(1)}, u32[]{:S(2)}, u32[]{:S(2)}) collective-permute-start(bf16[1,16,16,512]{3,2,1,0:T(8,128)(2,1)S(1)} %get-tuple-element.419), channel_id=1, source_target_pairs={{0,1},{1,2},{2,3},{3,4},{4,5},{5,6},{6,7},{7,8},{8,9},{9,10},{10,1... | collective-permute-start | bytes 786440 | tf_op jit(solution)/shard_map/while/body/eval_jaxpr/ppermute | solution.py:23
  305.7 6.1 %collective-permute-done.3 = bf16[1,16,16,512]{3,2,1,0:T(8,128)(2,1)} collective-permute-done((bf16[1,16,16,512]{3,2,1,0:T(8,128)(2,1)S(1)}, bf16[1,16,16,512]{3,2,1,0:T(8,128)(2,1)}, u32[]{:S(2)}, u32[]{:S(2)}) %collective-permute-start.3) | collective-permute-done | bytes 262176 | tf_op jit(solution)/shard_map/while/body/eval_jaxpr/ppermute | solution.py:25
  311.7 8.0 %conditional.7 = (bf16[1,16,16,512]{3,2,1,0:T(8,128)(2,1)}) conditional(s32[]{:T(128)} %convert_element_type.72, () %tuple.66, (bf16[1,16,16,512]{3,2,1,0:T(8,128)(2,1)S(1)}, bf16[1,16,16,512]{3,2,1,0:T(8,128)(2,1)S(1)}, bf16[9,512,512]{2,1,0:T(8,128)(2,1)}, bf16[1,16,16,512]{3,2,1,0:T(8,128)(2,1)S(1)}, bf16[3,512,512]{2,1,0:T(8,128)(2,1)S(1)}, ...), branch_computations={%region_3.3_spmd, %region_4.4_spmd} | conditional | flops 1612972032 | bytes 42729508 | solution.py:118
  312.0 1.5 fusion.33
  317.6 2.1 fusion.20
  322.0 4.3 %collective-permute-start.1 = (bf16[1,1,16,16,512]{4,3,2,1,0:T(8,128)(2,1)S(1)}, bf16[1,1,16,16,512]{4,3,2,1,0:T(8,128)(2,1)S(1)}, u32[]{:S(2)}, u32[]{:S(2)}) collective-permute-start(bf16[1,1,16,16,512]{4,3,2,1,0:T(8,128)(2,1)S(1)} %broadcast_select_fusion.3), channel_id=1, source_target_pairs={{0,16},{1,17},{2,18},{3,19},{4,20},{5,21},{6,22},{7,23},{8,24},{9,... | collective-permute-start | bytes 786440 | tf_op jit(solution)/shard_map/while/body/eval_jaxpr/ppermute | solution.py:12
  330.2 2.9 collective-permute-done
  333.1 2.0 fusion.72
  335.1 8.5 %collective-permute-start.2 = (bf16[1,16,16,512]{3,2,1,0:T(8,128)(2,1)S(1)}, bf16[1,16,16,512]{3,2,1,0:T(8,128)(2,1)S(1)}, u32[]{:S(2)}, u32[]{:S(2)}) collective-permute-start(bf16[1,16,16,512]{3,2,1,0:T(8,128)(2,1)S(1)} %get-tuple-element.419), channel_id=1, source_target_pairs={{0,1},{1,2},{2,3},{3,4},{4,5},{5,6},{6,7},{7,8},{8,9},{9,10},{10,1... | collective-permute-start | bytes 786440 | tf_op jit(solution)/shard_map/while/body/eval_jaxpr/ppermute | solution.py:23
  345.0 6.1 %collective-permute-done.3 = bf16[1,16,16,512]{3,2,1,0:T(8,128)(2,1)} collective-permute-done((bf16[1,16,16,512]{3,2,1,0:T(8,128)(2,1)S(1)}, bf16[1,16,16,512]{3,2,1,0:T(8,128)(2,1)}, u32[]{:S(2)}, u32[]{:S(2)}) %collective-permute-start.3) | collective-permute-done | bytes 262176 | tf_op jit(solution)/shard_map/while/body/eval_jaxpr/ppermute | solution.py:25
  354.2 66.0 %all-reduce.4.cloned.1.call-done = bf16[4,1,16,16,512]{4,3,2,1,0:T(8,128)(2,1)} async-done(((bf16[4,1,16,16,512]{4,3,2,1,0:T(8,128)(2,1)}), bf16[4,1,16,16,512]{4,3,2,1,0:T(8,128)(2,1)}) %all-reduce.4.cloned.1.call-update) | async-done | bytes 1048592 | tf_op jit(solution)/shard_map/psum | solution.py:34
  420.2 1.9 constant_dynamic-slice_fusion
  (170 shorter events, 75.4 us)
Async XLA Ops:
  6.5 45.4 %all-gather.8.cloned.1.call-start = ((), (), s32[]{:S(2)}) async-start(), calls=%async_computation.2 | async-start | bytes 1671168 | tf_op jit(solution)/shard_map/all_gather | solution.py:71
  7.3 98.5 %all-gather.4.cloned.1.call-start = ((), (), s32[]{:S(2)}) async-start(), calls=%async_computation | async-start | bytes 5013504 | tf_op jit(solution)/shard_map/all_gather | solution.py:69
  8.0 151.5 %all-gather.6.cloned.1.call-start = ((), (), s32[]{:S(2)}) async-start(), calls=%async_computation.1 | async-start | bytes 5013504 | tf_op jit(solution)/shard_map/all_gather | solution.py:70
  8.7 411.5 %all-reduce.4.cloned.1.call-start = ((), (), s32[]{:S(2)}) async-start(), calls=%async_computation.3 | async-start | bytes 2097152 | tf_op jit(solution)/shard_map/psum | solution.py:34
  160.3 10.1 %collective-permute-start.1 = (bf16[1,1,16,16,512]{4,3,2,1,0:T(8,128)(2,1)S(1)}, bf16[1,1,16,16,512]{4,3,2,1,0:T(8,128)(2,1)S(1)}, u32[]{:S(2)}, u32[]{:S(2)}) collective-permute-start(bf16[1,1,16,16,512]{4,3,2,1,0:T(8,128)(2,1)S(1)} %broadcast_select_fusion.3), channel_id=1, source_target_pairs={{0,16},{1,17},{2,18},{3,19},{4,20},{5,21},{6,22},{7,23},{8,24},{9,... | collective-permute-start | bytes 786440 | tf_op jit(solution)/shard_map/while/body/eval_jaxpr/ppermute | solution.py:12
  163.7 11.7 %collective-permute-start = (bf16[1,16,16,512]{3,2,1,0:T(8,128)(2,1)}, bf16[1,16,16,512]{3,2,1,0:T(8,128)(2,1)S(1)}, u32[]{:S(2)}, u32[]{:S(2)}) collective-permute-start(bf16[1,16,16,512]{3,2,1,0:T(8,128)(2,1)} %get-tuple-element.384), channel_id=1, source_target_pairs={{0,16},{1,17},{2,18},{3,19},{4,20},{5,21},{6,22},{7,23},{8,24},{9,... | collective-permute-start | bytes 786440 | tf_op jit(solution)/shard_map/while/body/eval_jaxpr/ppermute | solution.py:12
  175.3 13.0 %copy-start.2 = (bf16[3,512,512]{2,1,0:T(8,128)(2,1)S(1)}, bf16[3,512,512]{2,1,0:T(8,128)(2,1)}, u32[]{:S(2)}) copy-start(bf16[3,512,512]{2,1,0:T(8,128)(2,1)} %get-tuple-element.414) | copy-start | bytes 4718596 | tf_op jit(solution)/shard_map/while
  177.3 3.1 copy-start
  182.7 2.6 collective-permute-start.2
  184.1 4.3 %collective-permute-start.3 = (bf16[1,16,16,512]{3,2,1,0:T(8,128)(2,1)S(1)}, bf16[1,16,16,512]{3,2,1,0:T(8,128)(2,1)}, u32[]{:S(2)}, u32[]{:S(2)}) collective-permute-start(bf16[1,16,16,512]{3,2,1,0:T(8,128)(2,1)S(1)} %get-tuple-element.419), channel_id=1, source_target_pairs={{1,0},{2,1},{3,2},{4,3},{5,4},{6,5},{7,6},{8,7},{9,8},{10,9},{11,1... | collective-permute-start | bytes 786440 | tf_op jit(solution)/shard_map/while/body/eval_jaxpr/ppermute | solution.py:25
  188.4 3.1 copy-start.1
  198.7 5.2 %collective-permute-start.1 = (bf16[1,1,16,16,512]{4,3,2,1,0:T(8,128)(2,1)S(1)}, bf16[1,1,16,16,512]{4,3,2,1,0:T(8,128)(2,1)S(1)}, u32[]{:S(2)}, u32[]{:S(2)}) collective-permute-start(bf16[1,1,16,16,512]{4,3,2,1,0:T(8,128)(2,1)S(1)} %broadcast_select_fusion.3), channel_id=1, source_target_pairs={{0,16},{1,17},{2,18},{3,19},{4,20},{5,21},{6,22},{7,23},{8,24},{9,... | collective-permute-start | bytes 786440 | tf_op jit(solution)/shard_map/while/body/eval_jaxpr/ppermute | solution.py:12
  200.0 8.3 %collective-permute-start = (bf16[1,16,16,512]{3,2,1,0:T(8,128)(2,1)}, bf16[1,16,16,512]{3,2,1,0:T(8,128)(2,1)S(1)}, u32[]{:S(2)}, u32[]{:S(2)}) collective-permute-start(bf16[1,16,16,512]{3,2,1,0:T(8,128)(2,1)} %get-tuple-element.384), channel_id=1, source_target_pairs={{0,16},{1,17},{2,18},{3,19},{4,20},{5,21},{6,22},{7,23},{8,24},{9,... | collective-permute-start | bytes 786440 | tf_op jit(solution)/shard_map/while/body/eval_jaxpr/ppermute | solution.py:12
  208.3 17.9 %copy-start.2 = (bf16[3,512,512]{2,1,0:T(8,128)(2,1)S(1)}, bf16[3,512,512]{2,1,0:T(8,128)(2,1)}, u32[]{:S(2)}) copy-start(bf16[3,512,512]{2,1,0:T(8,128)(2,1)} %get-tuple-element.414) | copy-start | bytes 4718596 | tf_op jit(solution)/shard_map/while
  210.3 3.1 copy-start
  215.7 7.4 %collective-permute-start.2 = (bf16[1,16,16,512]{3,2,1,0:T(8,128)(2,1)S(1)}, bf16[1,16,16,512]{3,2,1,0:T(8,128)(2,1)S(1)}, u32[]{:S(2)}, u32[]{:S(2)}) collective-permute-start(bf16[1,16,16,512]{3,2,1,0:T(8,128)(2,1)S(1)} %get-tuple-element.419), channel_id=1, source_target_pairs={{0,1},{1,2},{2,3},{3,4},{4,5},{5,6},{6,7},{7,8},{8,9},{9,10},{10,1... | collective-permute-start | bytes 786440 | tf_op jit(solution)/shard_map/while/body/eval_jaxpr/ppermute | solution.py:23
  221.8 4.4 %collective-permute-start.3 = (bf16[1,16,16,512]{3,2,1,0:T(8,128)(2,1)S(1)}, bf16[1,16,16,512]{3,2,1,0:T(8,128)(2,1)}, u32[]{:S(2)}, u32[]{:S(2)}) collective-permute-start(bf16[1,16,16,512]{3,2,1,0:T(8,128)(2,1)S(1)} %get-tuple-element.419), channel_id=1, source_target_pairs={{1,0},{2,1},{3,2},{4,3},{5,4},{6,5},{7,6},{8,7},{9,8},{10,9},{11,1... | collective-permute-start | bytes 786440 | tf_op jit(solution)/shard_map/while/body/eval_jaxpr/ppermute | solution.py:25
  226.2 3.1 copy-start.1
  236.5 8.2 %collective-permute-start.1 = (bf16[1,1,16,16,512]{4,3,2,1,0:T(8,128)(2,1)S(1)}, bf16[1,1,16,16,512]{4,3,2,1,0:T(8,128)(2,1)S(1)}, u32[]{:S(2)}, u32[]{:S(2)}) collective-permute-start(bf16[1,1,16,16,512]{4,3,2,1,0:T(8,128)(2,1)S(1)} %broadcast_select_fusion.3), channel_id=1, source_target_pairs={{0,16},{1,17},{2,18},{3,19},{4,20},{5,21},{6,22},{7,23},{8,24},{9,... | collective-permute-start | bytes 786440 | tf_op jit(solution)/shard_map/while/body/eval_jaxpr/ppermute | solution.py:12
  240.8 7.5 %collective-permute-start = (bf16[1,16,16,512]{3,2,1,0:T(8,128)(2,1)}, bf16[1,16,16,512]{3,2,1,0:T(8,128)(2,1)S(1)}, u32[]{:S(2)}, u32[]{:S(2)}) collective-permute-start(bf16[1,16,16,512]{3,2,1,0:T(8,128)(2,1)} %get-tuple-element.384), channel_id=1, source_target_pairs={{0,16},{1,17},{2,18},{3,19},{4,20},{5,21},{6,22},{7,23},{8,24},{9,... | collective-permute-start | bytes 786440 | tf_op jit(solution)/shard_map/while/body/eval_jaxpr/ppermute | solution.py:12
  248.3 18.7 %copy-start.2 = (bf16[3,512,512]{2,1,0:T(8,128)(2,1)S(1)}, bf16[3,512,512]{2,1,0:T(8,128)(2,1)}, u32[]{:S(2)}) copy-start(bf16[3,512,512]{2,1,0:T(8,128)(2,1)} %get-tuple-element.414) | copy-start | bytes 4718596 | tf_op jit(solution)/shard_map/while
  250.3 3.1 copy-start
  255.7 8.2 %collective-permute-start.2 = (bf16[1,16,16,512]{3,2,1,0:T(8,128)(2,1)S(1)}, bf16[1,16,16,512]{3,2,1,0:T(8,128)(2,1)S(1)}, u32[]{:S(2)}, u32[]{:S(2)}) collective-permute-start(bf16[1,16,16,512]{3,2,1,0:T(8,128)(2,1)S(1)} %get-tuple-element.419), channel_id=1, source_target_pairs={{0,1},{1,2},{2,3},{3,4},{4,5},{5,6},{6,7},{7,8},{8,9},{9,10},{10,1... | collective-permute-start | bytes 786440 | tf_op jit(solution)/shard_map/while/body/eval_jaxpr/ppermute | solution.py:23
  262.6 4.4 %collective-permute-start.3 = (bf16[1,16,16,512]{3,2,1,0:T(8,128)(2,1)S(1)}, bf16[1,16,16,512]{3,2,1,0:T(8,128)(2,1)}, u32[]{:S(2)}, u32[]{:S(2)}) collective-permute-start(bf16[1,16,16,512]{3,2,1,0:T(8,128)(2,1)S(1)} %get-tuple-element.419), channel_id=1, source_target_pairs={{1,0},{2,1},{3,2},{4,3},{5,4},{6,5},{7,6},{8,7},{9,8},{10,9},{11,1... | collective-permute-start | bytes 786440 | tf_op jit(solution)/shard_map/while/body/eval_jaxpr/ppermute | solution.py:25
  267.0 3.1 copy-start.1
  277.3 8.2 %collective-permute-start.1 = (bf16[1,1,16,16,512]{4,3,2,1,0:T(8,128)(2,1)S(1)}, bf16[1,1,16,16,512]{4,3,2,1,0:T(8,128)(2,1)S(1)}, u32[]{:S(2)}, u32[]{:S(2)}) collective-permute-start(bf16[1,1,16,16,512]{4,3,2,1,0:T(8,128)(2,1)S(1)} %broadcast_select_fusion.3), channel_id=1, source_target_pairs={{0,16},{1,17},{2,18},{3,19},{4,20},{5,21},{6,22},{7,23},{8,24},{9,... | collective-permute-start | bytes 786440 | tf_op jit(solution)/shard_map/while/body/eval_jaxpr/ppermute | solution.py:12
  281.6 6.8 %collective-permute-start = (bf16[1,16,16,512]{3,2,1,0:T(8,128)(2,1)}, bf16[1,16,16,512]{3,2,1,0:T(8,128)(2,1)S(1)}, u32[]{:S(2)}, u32[]{:S(2)}) collective-permute-start(bf16[1,16,16,512]{3,2,1,0:T(8,128)(2,1)} %get-tuple-element.384), channel_id=1, source_target_pairs={{0,16},{1,17},{2,18},{3,19},{4,20},{5,21},{6,22},{7,23},{8,24},{9,... | collective-permute-start | bytes 786440 | tf_op jit(solution)/shard_map/while/body/eval_jaxpr/ppermute | solution.py:12
  288.4 23.3 %copy-start.2 = (bf16[3,512,512]{2,1,0:T(8,128)(2,1)S(1)}, bf16[3,512,512]{2,1,0:T(8,128)(2,1)}, u32[]{:S(2)}) copy-start(bf16[3,512,512]{2,1,0:T(8,128)(2,1)} %get-tuple-element.414) | copy-start | bytes 4718596 | tf_op jit(solution)/shard_map/while
  290.3 3.1 copy-start
  295.8 9.9 %collective-permute-start.2 = (bf16[1,16,16,512]{3,2,1,0:T(8,128)(2,1)S(1)}, bf16[1,16,16,512]{3,2,1,0:T(8,128)(2,1)S(1)}, u32[]{:S(2)}, u32[]{:S(2)}) collective-permute-start(bf16[1,16,16,512]{3,2,1,0:T(8,128)(2,1)S(1)} %get-tuple-element.419), channel_id=1, source_target_pairs={{0,1},{1,2},{2,3},{3,4},{4,5},{5,6},{6,7},{7,8},{8,9},{9,10},{10,1... | collective-permute-start | bytes 786440 | tf_op jit(solution)/shard_map/while/body/eval_jaxpr/ppermute | solution.py:23
  304.3 7.4 %collective-permute-start.3 = (bf16[1,16,16,512]{3,2,1,0:T(8,128)(2,1)S(1)}, bf16[1,16,16,512]{3,2,1,0:T(8,128)(2,1)}, u32[]{:S(2)}, u32[]{:S(2)}) collective-permute-start(bf16[1,16,16,512]{3,2,1,0:T(8,128)(2,1)S(1)} %get-tuple-element.419), channel_id=1, source_target_pairs={{1,0},{2,1},{3,2},{4,3},{5,4},{6,5},{7,6},{8,7},{9,8},{10,9},{11,1... | collective-permute-start | bytes 786440 | tf_op jit(solution)/shard_map/while/body/eval_jaxpr/ppermute | solution.py:25
  311.7 3.1 copy-start.1
  322.0 8.2 %collective-permute-start.1 = (bf16[1,1,16,16,512]{4,3,2,1,0:T(8,128)(2,1)S(1)}, bf16[1,1,16,16,512]{4,3,2,1,0:T(8,128)(2,1)S(1)}, u32[]{:S(2)}, u32[]{:S(2)}) collective-permute-start(bf16[1,1,16,16,512]{4,3,2,1,0:T(8,128)(2,1)S(1)} %broadcast_select_fusion.3), channel_id=1, source_target_pairs={{0,16},{1,17},{2,18},{3,19},{4,20},{5,21},{6,22},{7,23},{8,24},{9,... | collective-permute-start | bytes 786440 | tf_op jit(solution)/shard_map/while/body/eval_jaxpr/ppermute | solution.py:12
  326.3 6.8 %collective-permute-start = (bf16[1,16,16,512]{3,2,1,0:T(8,128)(2,1)}, bf16[1,16,16,512]{3,2,1,0:T(8,128)(2,1)S(1)}, u32[]{:S(2)}, u32[]{:S(2)}) collective-permute-start(bf16[1,16,16,512]{3,2,1,0:T(8,128)(2,1)} %get-tuple-element.384), channel_id=1, source_target_pairs={{0,16},{1,17},{2,18},{3,19},{4,20},{5,21},{6,22},{7,23},{8,24},{9,... | collective-permute-start | bytes 786440 | tf_op jit(solution)/shard_map/while/body/eval_jaxpr/ppermute | solution.py:12
  333.1 17.9 %copy-start.2 = (bf16[3,512,512]{2,1,0:T(8,128)(2,1)S(1)}, bf16[3,512,512]{2,1,0:T(8,128)(2,1)}, u32[]{:S(2)}) copy-start(bf16[3,512,512]{2,1,0:T(8,128)(2,1)} %get-tuple-element.414) | copy-start | bytes 4718596 | tf_op jit(solution)/shard_map/while
  335.1 9.9 %collective-permute-start.2 = (bf16[1,16,16,512]{3,2,1,0:T(8,128)(2,1)S(1)}, bf16[1,16,16,512]{3,2,1,0:T(8,128)(2,1)S(1)}, u32[]{:S(2)}, u32[]{:S(2)}) collective-permute-start(bf16[1,16,16,512]{3,2,1,0:T(8,128)(2,1)S(1)} %get-tuple-element.419), channel_id=1, source_target_pairs={{0,1},{1,2},{2,3},{3,4},{4,5},{5,6},{6,7},{7,8},{8,9},{9,10},{10,1... | collective-permute-start | bytes 786440 | tf_op jit(solution)/shard_map/while/body/eval_jaxpr/ppermute | solution.py:23
  343.6 7.4 %collective-permute-start.3 = (bf16[1,16,16,512]{3,2,1,0:T(8,128)(2,1)S(1)}, bf16[1,16,16,512]{3,2,1,0:T(8,128)(2,1)}, u32[]{:S(2)}, u32[]{:S(2)}) collective-permute-start(bf16[1,16,16,512]{3,2,1,0:T(8,128)(2,1)S(1)} %get-tuple-element.419), channel_id=1, source_target_pairs={{1,0},{2,1},{3,2},{4,3},{5,4},{6,5},{7,6},{8,7},{9,8},{10,9},{11,1... | collective-permute-start | bytes 786440 | tf_op jit(solution)/shard_map/while/body/eval_jaxpr/ppermute | solution.py:25
Sparse Core Ops, SparseCore 0:
  9.5 42.3 all-gather.7
  54.1 51.6 all-gather.3
  108.0 51.4 all-gather.5
  354.3 65.8 all-reduce.3
where the time goes:
time: 430 us; the launch traced here: 429 us
  waiting for transfers between devices  268 us (62%)
  starting transfers between devices  62.1 us (14%)
  matrix products  50 us (12%)
  other arithmetic  22 us (5%)
  between operations  13.2 us (3%)
  local copies, waits for them, and re-layouts  8.96 us (2%)
  loops' own time  4.66 us (1%)
    psum x1, waiting for transfers between devices, broadcast(): return lax.psum(jnp.where(mine, shard, jnp.zeros_like(shard)), axis)  66 us
    all_gather x1, waiting for transfers between devices, on_device(): lax.all_gather(conv_first, 'frame', axis=2, tiled=True)  53.9 us
    all_gather x1, waiting for transfers between devices, on_device(): lax.all_gather(conv_second, 'frame', axis=2, tiled=True)  53.7 us
    all_gather x1, waiting for transfers between devices, on_device(): lax.all_gather(temporal, 'frame', axis=2, tiled=True)  43.1 us
    dot_general x72, matrix products, spatial(): jnp.dot(window, kernel[3 * row_shift + col_shift], preferred_element_type...  39.4 us
    ppermute x5, starting transfers between devices, extended_2(): lax.ppermute(tail, axis, [(i, (i + 1) % count) for i in range(ends)])  31.4 us
    ppermute x10, waiting for transfers between devices, passed_along(): return lax.ppermute(shard, axis, pairs)  27.6 us
    ppermute x10, starting transfers between devices, passed_along(): return lax.ppermute(shard, axis, pairs)  24.1 us
  transfers between devices with their start and end apart: 24, of which 19 were waited for; matrix products, arithmetic and copies ran while one was open for 1% of the time, Pallas kernels for 0%

commit v1 on v0

--- a/solution.py
+++ b/solution.py
@@ -65,8 +65,11 @@
 def on_device(noisy_clips, conv_first, conv_second, temporal):
     sections = lax.axis_size("segment")
     segment_id = lax.axis_index("segment")
+    map_the_arrays = lambda my_tile, bus_axis: jnp.concatenate(
+        lax.all_gather(my_tile, bus_axis), axis=2
+    )
     first_full, second_full, time_full = (
-        lax.all_gather(conv_first, "frame", axis=2, tiled=True),
+        map_the_arrays(conv_first, "frame"),
         lax.all_gather(conv_second, "frame", axis=2, tiled=True),
         lax.all_gather(temporal, "frame", axis=2, tiled=True),
     )

time: 430 us -> 430 us (level)
  local copies, waits for them, and re-layouts: 8.96 us -> 13.8 us
    all_gather x1, waiting for transfers between devices: 43.1 us -> 35.2 us  [on_device(): lax.all_gather(temporal, 'frame', axis=2, tiled=True)]
    all_gather x0 -> x1, local copies, waits for them, and re-layouts: none -> 5.23 us  [on_device(): lax.all_gather(my_tile, bus_axis)]
  transfers between devices with their start and end apart: 24 -> 24, of which waited for: 19 -> 19; matrix products, arithmetic and copies ran while one was open for 1% -> 2% of each run, Pallas kernels for 0% -> 0%
where the time goes in v1:
time: 430 us; the launch traced here: 429 us
  waiting for transfers between devices  264 us (61%)
  starting transfers between devices  62.1 us (14%)
  matrix products  50 us (12%)
  other arithmetic  22 us (5%)
  local copies, waits for them, and re-layouts  13.8 us (3%)
  between operations  13.2 us (3%)
    psum x1, waiting for transfers between devices, broadcast(): return lax.psum(jnp.where(mine, shard, jnp.zeros_like(shard)), axis)  66 us
    all_gather x1, waiting for transfers between devices, on_device(): lax.all_gather(my_tile, bus_axis)  56.7 us
    all_gather x1, waiting for transfers between devices, on_device(): lax.all_gather(conv_second, 'frame', axis=2, tiled=True)  53.9 us
    dot_general x72, matrix products, spatial(): jnp.dot(window, kernel[3 * row_shift + col_shift], preferred_element_type...  39.3 us
    all_gather x1, waiting for transfers between devices, on_device(): lax.all_gather(temporal, 'frame', axis=2, tiled=True)  35.2 us
    ppermute x5, starting transfers between devices, extended_2(): lax.ppermute(tail, axis, [(i, (i + 1) % count) for i in range(ends)])  31.4 us
    ppermute x10, waiting for transfers between devices, passed_along(): return lax.ppermute(shard, axis, pairs)  28.7 us
    ppermute x10, starting transfers between devices, passed_along(): return lax.ppermute(shard, axis, pairs)  24.1 us
  transfers between devices with their start and end apart: 24, of which 19 were waited for; matrix products, arithmetic and copies ran while one was open for 2% of the time, Pallas kernels for 0%

profile of v1, /device:TPU:0, one launch (start us, length us, event | category | flops | bytes accessed | tf_op | source)
XLA Modules:
  0.0 428.8 jit_solution(4717403278546231856)
XLA Ops:
  8.8 56.7 %all-gather.9.cloned.1.call-done = bf16[16,9,32,512]{3,2,1,0:T(8,128)(2,1)} async-done(((bf16[1,9,32,512]{3,2,1,0:T(8,128)(2,1)}), bf16[16,9,32,512]{3,2,1,0:T(8,128)(2,1)}) %all-gather.9.cloned.1.call-update) | async-done | bytes 4718608 | tf_op jit(solution)/shard_map/all_gather | solution.py:69
  65.5 5.2 %copy.6 = bf16[16,9,32,512]{3,2,0,1:T(8,128)(2,1)} copy(bf16[16,9,32,512]{3,2,1,0:T(8,128)(2,1)} %all-gather.9.cloned.1.call-done) | data formatting | bytes 9437184 | tf_op jit(solution)/shard_map/all_gather | solution.py:69
  70.7 35.2 %all-gather.7.cloned.1.call-done = bf16[1,3,512,512]{3,2,1,0:T(8,128)(2,1)} async-done(((bf16[1,3,32,512]{3,2,1,0:T(8,128)(2,1)}), bf16[1,3,512,512]{3,2,1,0:T(8,128)(2,1)}) %all-gather.7.cloned.1.call-update) | async-done | bytes 1572880 | tf_op jit(solution)/shard_map/all_gather | solution.py:74
  105.9 53.9 %all-gather.5.cloned.1.call-done = bf16[1,9,512,512]{3,2,1,0:T(8,128)(2,1)} async-done(((bf16[1,9,32,512]{3,2,1,0:T(8,128)(2,1)}), bf16[1,9,512,512]{3,2,1,0:T(8,128)(2,1)}) %all-gather.5.cloned.1.call-update) | async-done | bytes 4718608 | tf_op jit(solution)/shard_map/all_gather | solution.py:73
  160.5 192.8 %while.17 = (s32[]{:T(128)}, bf16[1,16,16,512]{3,2,1,0:T(8,128)(2,1)}, bf16[1,1,16,16,512]{4,3,2,1,0:T(8,128)(2,1)}, bf16[4,1,16,16,512]{4,3,2,1,0:T(8,128)(2,1)...) while((s32[]{:T(128)}, ...), condition=%wide.region_5.6_spmd.clone, body=%wide.region_0.5_spmd.clone.sunk | while | flops 2824994816 | bytes 95421016 | solution.py:126
  160.5 3.4 collective-permute-start.1
  166.4 4.2 collective-permute-done.1
  170.6 5.0 %collective-permute-done = bf16[1,16,16,512]{3,2,1,0:T(8,128)(2,1)S(1)} collective-permute-done((bf16[1,16,16,512]{3,2,1,0:T(8,128)(2,1)}, bf16[1,16,16,512]{3,2,1,0:T(8,128)(2,1)S(1)}, u32[]{:S(2)}, u32[]{:S(2)}) %collective-permute-start) | collective-permute-done | bytes 262176 | tf_op jit(solution)/shard_map/while/body/eval_jaxpr/ppermute | solution.py:12
  175.6 1.9 fusion.72
  177.6 5.4 %conditional.6 = (bf16[1,16,16,512]{3,2,1,0:T(8,128)(2,1)S(1)}) conditional(s32[]{:T(128)} %convert_element_type.72, () %tuple.67, (bf16[1,16,16,512]{3,2,1,0:T(8,128)(2,1)S(1)}, bf16[9,512,512]{2,1,0:T(8,128)(2,1)}) %tuple.68), branch_computations={%region_1.1_spmd, %region_2.2_spmd} | conditional | flops 1209663488 | bytes 38010916 | solution.py:108
  185.6 3.0 collective-permute-done.3
  188.7 8.0 %conditional.7 = (bf16[1,16,16,512]{3,2,1,0:T(8,128)(2,1)}) conditional(s32[]{:T(128)} %convert_element_type.72, () %tuple.66, (bf16[1,16,16,512]{3,2,1,0:T(8,128)(2,1)S(1)}, bf16[1,16,16,512]{3,2,1,0:T(8,128)(2,1)S(1)}, bf16[9,512,512]{2,1,0:T(8,128)(2,1)}, bf16[1,16,16,512]{3,2,1,0:T(8,128)(2,1)S(1)}, bf16[3,512,512]{2,1,0:T(8,128)(2,1)S(1)}, ...), branch_computations={%region_3.3_spmd, %region_4.4_spmd} | conditional | flops 1612972032 | bytes 42729508 | solution.py:121
  188.9 1.5 fusion.33
  194.5 2.1 fusion.20
  204.1 4.5 %collective-permute-done = bf16[1,16,16,512]{3,2,1,0:T(8,128)(2,1)S(1)} collective-permute-done((bf16[1,16,16,512]{3,2,1,0:T(8,128)(2,1)}, bf16[1,16,16,512]{3,2,1,0:T(8,128)(2,1)S(1)}, u32[]{:S(2)}, u32[]{:S(2)}) %collective-permute-start) | collective-permute-done | bytes 262176 | tf_op jit(solution)/shard_map/while/body/eval_jaxpr/ppermute | solution.py:12
  208.6 1.9 fusion.72
  210.5 5.4 %conditional.6 = (bf16[1,16,16,512]{3,2,1,0:T(8,128)(2,1)S(1)}) conditional(s32[]{:T(128)} %convert_element_type.72, () %tuple.67, (bf16[1,16,16,512]{3,2,1,0:T(8,128)(2,1)S(1)}, bf16[9,512,512]{2,1,0:T(8,128)(2,1)}) %tuple.68), branch_computations={%region_1.1_spmd, %region_2.2_spmd} | conditional | flops 1209663488 | bytes 38010916 | solution.py:108
  210.8 1.5 fusion.8
  216.0 6.1 %collective-permute-start.2 = (bf16[1,16,16,512]{3,2,1,0:T(8,128)(2,1)S(1)}, bf16[1,16,16,512]{3,2,1,0:T(8,128)(2,1)S(1)}, u32[]{:S(2)}, u32[]{:S(2)}) collective-permute-start(bf16[1,16,16,512]{3,2,1,0:T(8,128)(2,1)S(1)} %get-tuple-element.419), channel_id=1, source_target_pairs={{0,1},{1,2},{2,3},{3,4},{4,5},{5,6},{6,7},{7,8},{8,9},{9,10},{10,1... | collective-permute-start | bytes 786440 | tf_op jit(solution)/shard_map/while/body/eval_jaxpr/ppermute | solution.py:23
  223.4 3.1 collective-permute-done.3
  226.5 8.0 %conditional.7 = (bf16[1,16,16,512]{3,2,1,0:T(8,128)(2,1)}) conditional(s32[]{:T(128)} %convert_element_type.72, () %tuple.66, (bf16[1,16,16,512]{3,2,1,0:T(8,128)(2,1)S(1)}, bf16[1,16,16,512]{3,2,1,0:T(8,128)(2,1)S(1)}, bf16[9,512,512]{2,1,0:T(8,128)(2,1)}, bf16[1,16,16,512]{3,2,1,0:T(8,128)(2,1)S(1)}, bf16[3,512,512]{2,1,0:T(8,128)(2,1)S(1)}, ...), branch_computations={%region_3.3_spmd, %region_4.4_spmd} | conditional | flops 1612972032 | bytes 42729508 | solution.py:121
  232.4 2.1 fusion.20
  236.7 4.3 %collective-permute-start.1 = (bf16[1,1,16,16,512]{4,3,2,1,0:T(8,128)(2,1)S(1)}, bf16[1,1,16,16,512]{4,3,2,1,0:T(8,128)(2,1)S(1)}, u32[]{:S(2)}, u32[]{:S(2)}) collective-permute-start(bf16[1,1,16,16,512]{4,3,2,1,0:T(8,128)(2,1)S(1)} %broadcast_select_fusion.3), channel_id=1, source_target_pairs={{0,16},{1,17},{2,18},{3,19},{4,20},{5,21},{6,22},{7,23},{8,24},{9,... | collective-permute-start | bytes 786440 | tf_op jit(solution)/shard_map/while/body/eval_jaxpr/ppermute | solution.py:12
  244.9 3.7 collective-permute-done
  248.6 1.9 fusion.72
  250.5 5.4 %conditional.6 = (bf16[1,16,16,512]{3,2,1,0:T(8,128)(2,1)S(1)}) conditional(s32[]{:T(128)} %convert_element_type.72, () %tuple.67, (bf16[1,16,16,512]{3,2,1,0:T(8,128)(2,1)S(1)}, bf16[9,512,512]{2,1,0:T(8,128)(2,1)}) %tuple.68), branch_computations={%region_1.1_spmd, %region_2.2_spmd} | conditional | flops 1209663488 | bytes 38010916 | solution.py:108
  256.0 6.9 %collective-permute-start.2 = (bf16[1,16,16,512]{3,2,1,0:T(8,128)(2,1)S(1)}, bf16[1,16,16,512]{3,2,1,0:T(8,128)(2,1)S(1)}, u32[]{:S(2)}, u32[]{:S(2)}) collective-permute-start(bf16[1,16,16,512]{3,2,1,0:T(8,128)(2,1)S(1)} %get-tuple-element.419), channel_id=1, source_target_pairs={{0,1},{1,2},{2,3},{3,4},{4,5},{5,6},{6,7},{7,8},{8,9},{9,10},{10,1... | collective-permute-start | bytes 786440 | tf_op jit(solution)/shard_map/while/body/eval_jaxpr/ppermute | solution.py:23
  264.2 3.1 collective-permute-done.3
  267.3 8.0 %conditional.7 = (bf16[1,16,16,512]{3,2,1,0:T(8,128)(2,1)}) conditional(s32[]{:T(128)} %convert_element_type.72, () %tuple.66, (bf16[1,16,16,512]{3,2,1,0:T(8,128)(2,1)S(1)}, bf16[1,16,16,512]{3,2,1,0:T(8,128)(2,1)S(1)}, bf16[9,512,512]{2,1,0:T(8,128)(2,1)}, bf16[1,16,16,512]{3,2,1,0:T(8,128)(2,1)S(1)}, bf16[3,512,512]{2,1,0:T(8,128)(2,1)S(1)}, ...), branch_computations={%region_3.3_spmd, %region_4.4_spmd} | conditional | flops 1612972032 | bytes 42729508 | solution.py:121
  267.6 1.5 fusion.33
  273.2 2.1 fusion.20
  277.5 4.3 %collective-permute-start.1 = (bf16[1,1,16,16,512]{4,3,2,1,0:T(8,128)(2,1)S(1)}, bf16[1,1,16,16,512]{4,3,2,1,0:T(8,128)(2,1)S(1)}, u32[]{:S(2)}, u32[]{:S(2)}) collective-permute-start(bf16[1,1,16,16,512]{4,3,2,1,0:T(8,128)(2,1)S(1)} %broadcast_select_fusion.3), channel_id=1, source_target_pairs={{0,16},{1,17},{2,18},{3,19},{4,20},{5,21},{6,22},{7,23},{8,24},{9,... | collective-permute-start | bytes 786440 | tf_op jit(solution)/shard_map/while/body/eval_jaxpr/ppermute | solution.py:12
  285.7 2.9 collective-permute-done
  288.6 1.9 fusion.72
  290.6 5.4 %conditional.6 = (bf16[1,16,16,512]{3,2,1,0:T(8,128)(2,1)S(1)}) conditional(s32[]{:T(128)} %convert_element_type.72, () %tuple.67, (bf16[1,16,16,512]{3,2,1,0:T(8,128)(2,1)S(1)}, bf16[9,512,512]{2,1,0:T(8,128)(2,1)}) %tuple.68), branch_computations={%region_1.1_spmd, %region_2.2_spmd} | conditional | flops 1209663488 | bytes 38010916 | solution.py:108
  290.9 1.5 fusion.8
  296.0 8.5 %collective-permute-start.2 = (bf16[1,16,16,512]{3,2,1,0:T(8,128)(2,1)S(1)}, bf16[1,16,16,512]{3,2,1,0:T(8,128)(2,1)S(1)}, u32[]{:S(2)}, u32[]{:S(2)}) collective-permute-start(bf16[1,16,16,512]{3,2,1,0:T(8,128)(2,1)S(1)} %get-tuple-element.419), channel_id=1, source_target_pairs={{0,1},{1,2},{2,3},{3,4},{4,5},{5,6},{6,7},{7,8},{8,9},{9,10},{10,1... | collective-permute-start | bytes 786440 | tf_op jit(solution)/shard_map/while/body/eval_jaxpr/ppermute | solution.py:23
  305.9 6.1 %collective-permute-done.3 = bf16[1,16,16,512]{3,2,1,0:T(8,128)(2,1)} collective-permute-done((bf16[1,16,16,512]{3,2,1,0:T(8,128)(2,1)S(1)}, bf16[1,16,16,512]{3,2,1,0:T(8,128)(2,1)}, u32[]{:S(2)}, u32[]{:S(2)}) %collective-permute-start.3) | collective-permute-done | bytes 262176 | tf_op jit(solution)/shard_map/while/body/eval_jaxpr/ppermute | solution.py:25
  312.0 8.0 %conditional.7 = (bf16[1,16,16,512]{3,2,1,0:T(8,128)(2,1)}) conditional(s32[]{:T(128)} %convert_element_type.72, () %tuple.66, (bf16[1,16,16,512]{3,2,1,0:T(8,128)(2,1)S(1)}, bf16[1,16,16,512]{3,2,1,0:T(8,128)(2,1)S(1)}, bf16[9,512,512]{2,1,0:T(8,128)(2,1)}, bf16[1,16,16,512]{3,2,1,0:T(8,128)(2,1)S(1)}, bf16[3,512,512]{2,1,0:T(8,128)(2,1)S(1)}, ...), branch_computations={%region_3.3_spmd, %region_4.4_spmd} | conditional | flops 1612972032 | bytes 42729508 | solution.py:121
  312.3 1.5 fusion.33
  317.9 2.1 fusion.20
  322.2 4.3 %collective-permute-start.1 = (bf16[1,1,16,16,512]{4,3,2,1,0:T(8,128)(2,1)S(1)}, bf16[1,1,16,16,512]{4,3,2,1,0:T(8,128)(2,1)S(1)}, u32[]{:S(2)}, u32[]{:S(2)}) collective-permute-start(bf16[1,1,16,16,512]{4,3,2,1,0:T(8,128)(2,1)S(1)} %broadcast_select_fusion.3), channel_id=1, source_target_pairs={{0,16},{1,17},{2,18},{3,19},{4,20},{5,21},{6,22},{7,23},{8,24},{9,... | collective-permute-start | bytes 786440 | tf_op jit(solution)/shard_map/while/body/eval_jaxpr/ppermute | solution.py:12
  330.4 2.9 collective-permute-done
  333.3 1.9 fusion.72
  335.3 8.5 %collective-permute-start.2 = (bf16[1,16,16,512]{3,2,1,0:T(8,128)(2,1)S(1)}, bf16[1,16,16,512]{3,2,1,0:T(8,128)(2,1)S(1)}, u32[]{:S(2)}, u32[]{:S(2)}) collective-permute-start(bf16[1,16,16,512]{3,2,1,0:T(8,128)(2,1)S(1)} %get-tuple-element.419), channel_id=1, source_target_pairs={{0,1},{1,2},{2,3},{3,4},{4,5},{5,6},{6,7},{7,8},{8,9},{9,10},{10,1... | collective-permute-start | bytes 786440 | tf_op jit(solution)/shard_map/while/body/eval_jaxpr/ppermute | solution.py:23
  345.2 6.1 %collective-permute-done.3 = bf16[1,16,16,512]{3,2,1,0:T(8,128)(2,1)} collective-permute-done((bf16[1,16,16,512]{3,2,1,0:T(8,128)(2,1)S(1)}, bf16[1,16,16,512]{3,2,1,0:T(8,128)(2,1)}, u32[]{:S(2)}, u32[]{:S(2)}) %collective-permute-start.3) | collective-permute-done | bytes 262176 | tf_op jit(solution)/shard_map/while/body/eval_jaxpr/ppermute | solution.py:25
  354.4 66.0 %all-reduce.4.cloned.1.call-done = bf16[4,1,16,16,512]{4,3,2,1,0:T(8,128)(2,1)} async-done(((bf16[4,1,16,16,512]{4,3,2,1,0:T(8,128)(2,1)}), bf16[4,1,16,16,512]{4,3,2,1,0:T(8,128)(2,1)}) %all-reduce.4.cloned.1.call-update) | async-done | bytes 1048592 | tf_op jit(solution)/shard_map/psum | solution.py:34
  420.4 1.9 constant_dynamic-slice_fusion
  (171 shorter events, 77.3 us)
Async XLA Ops:
  6.5 59.0 %all-gather.9.cloned.1.call-start = ((), (), s32[]{:S(2)}) async-start(), calls=%async_computation.3 | async-start | bytes 5013504 | tf_op jit(solution)/shard_map/all_gather | solution.py:69
  7.3 98.6 %all-gather.7.cloned.1.call-start = ((), (), s32[]{:S(2)}) async-start(), calls=%async_computation.1 | async-start | bytes 1671168 | tf_op jit(solution)/shard_map/all_gather | solution.py:74
  8.0 151.8 %all-gather.5.cloned.1.call-start = ((), (), s32[]{:S(2)}) async-start(), calls=%async_computation | async-start | bytes 5013504 | tf_op jit(solution)/shard_map/all_gather | solution.py:73
  8.7 411.7 %all-reduce.4.cloned.1.call-start = ((), (), s32[]{:S(2)}) async-start(), calls=%async_computation.2 | async-start | bytes 2097152 | tf_op jit(solution)/shard_map/psum | solution.py:34
  160.5 10.1 %collective-permute-start.1 = (bf16[1,1,16,16,512]{4,3,2,1,0:T(8,128)(2,1)S(1)}, bf16[1,1,16,16,512]{4,3,2,1,0:T(8,128)(2,1)S(1)}, u32[]{:S(2)}, u32[]{:S(2)}) collective-permute-start(bf16[1,1,16,16,512]{4,3,2,1,0:T(8,128)(2,1)S(1)} %broadcast_select_fusion.3), channel_id=1, source_target_pairs={{0,16},{1,17},{2,18},{3,19},{4,20},{5,21},{6,22},{7,23},{8,24},{9,... | collective-permute-start | bytes 786440 | tf_op jit(solution)/shard_map/while/body/eval_jaxpr/ppermute | solution.py:12
  163.9 11.7 %collective-permute-start = (bf16[1,16,16,512]{3,2,1,0:T(8,128)(2,1)}, bf16[1,16,16,512]{3,2,1,0:T(8,128)(2,1)S(1)}, u32[]{:S(2)}, u32[]{:S(2)}) collective-permute-start(bf16[1,16,16,512]{3,2,1,0:T(8,128)(2,1)} %get-tuple-element.384), channel_id=1, source_target_pairs={{0,16},{1,17},{2,18},{3,19},{4,20},{5,21},{6,22},{7,23},{8,24},{9,... | collective-permute-start | bytes 786440 | tf_op jit(solution)/shard_map/while/body/eval_jaxpr/ppermute | solution.py:12
  175.6 13.0 %copy-start.2 = (bf16[3,512,512]{2,1,0:T(8,128)(2,1)S(1)}, bf16[3,512,512]{2,1,0:T(8,128)(2,1)}, u32[]{:S(2)}) copy-start(bf16[3,512,512]{2,1,0:T(8,128)(2,1)} %get-tuple-element.414) | copy-start | bytes 4718596 | tf_op jit(solution)/shard_map/while
  177.6 3.1 copy-start
  183.0 2.6 collective-permute-start.2
  184.3 4.3 %collective-permute-start.3 = (bf16[1,16,16,512]{3,2,1,0:T(8,128)(2,1)S(1)}, bf16[1,16,16,512]{3,2,1,0:T(8,128)(2,1)}, u32[]{:S(2)}, u32[]{:S(2)}) collective-permute-start(bf16[1,16,16,512]{3,2,1,0:T(8,128)(2,1)S(1)} %get-tuple-element.419), channel_id=1, source_target_pairs={{1,0},{2,1},{3,2},{4,3},{5,4},{6,5},{7,6},{8,7},{9,8},{10,9},{11,1... | collective-permute-start | bytes 786440 | tf_op jit(solution)/shard_map/while/body/eval_jaxpr/ppermute | solution.py:25
  188.7 3.1 copy-start.1
  198.9 5.2 %collective-permute-start.1 = (bf16[1,1,16,16,512]{4,3,2,1,0:T(8,128)(2,1)S(1)}, bf16[1,1,16,16,512]{4,3,2,1,0:T(8,128)(2,1)S(1)}, u32[]{:S(2)}, u32[]{:S(2)}) collective-permute-start(bf16[1,1,16,16,512]{4,3,2,1,0:T(8,128)(2,1)S(1)} %broadcast_select_fusion.3), channel_id=1, source_target_pairs={{0,16},{1,17},{2,18},{3,19},{4,20},{5,21},{6,22},{7,23},{8,24},{9,... | collective-permute-start | bytes 786440 | tf_op jit(solution)/shard_map/while/body/eval_jaxpr/ppermute | solution.py:12
  200.2 8.3 %collective-permute-start = (bf16[1,16,16,512]{3,2,1,0:T(8,128)(2,1)}, bf16[1,16,16,512]{3,2,1,0:T(8,128)(2,1)S(1)}, u32[]{:S(2)}, u32[]{:S(2)}) collective-permute-start(bf16[1,16,16,512]{3,2,1,0:T(8,128)(2,1)} %get-tuple-element.384), channel_id=1, source_target_pairs={{0,16},{1,17},{2,18},{3,19},{4,20},{5,21},{6,22},{7,23},{8,24},{9,... | collective-permute-start | bytes 786440 | tf_op jit(solution)/shard_map/while/body/eval_jaxpr/ppermute | solution.py:12
  208.6 17.9 %copy-start.2 = (bf16[3,512,512]{2,1,0:T(8,128)(2,1)S(1)}, bf16[3,512,512]{2,1,0:T(8,128)(2,1)}, u32[]{:S(2)}) copy-start(bf16[3,512,512]{2,1,0:T(8,128)(2,1)} %get-tuple-element.414) | copy-start | bytes 4718596 | tf_op jit(solution)/shard_map/while
  210.5 3.1 copy-start
  216.0 7.4 %collective-permute-start.2 = (bf16[1,16,16,512]{3,2,1,0:T(8,128)(2,1)S(1)}, bf16[1,16,16,512]{3,2,1,0:T(8,128)(2,1)S(1)}, u32[]{:S(2)}, u32[]{:S(2)}) collective-permute-start(bf16[1,16,16,512]{3,2,1,0:T(8,128)(2,1)S(1)} %get-tuple-element.419), channel_id=1, source_target_pairs={{0,1},{1,2},{2,3},{3,4},{4,5},{5,6},{6,7},{7,8},{8,9},{9,10},{10,1... | collective-permute-start | bytes 786440 | tf_op jit(solution)/shard_map/while/body/eval_jaxpr/ppermute | solution.py:23
  222.1 4.4 %collective-permute-start.3 = (bf16[1,16,16,512]{3,2,1,0:T(8,128)(2,1)S(1)}, bf16[1,16,16,512]{3,2,1,0:T(8,128)(2,1)}, u32[]{:S(2)}, u32[]{:S(2)}) collective-permute-start(bf16[1,16,16,512]{3,2,1,0:T(8,128)(2,1)S(1)} %get-tuple-element.419), channel_id=1, source_target_pairs={{1,0},{2,1},{3,2},{4,3},{5,4},{6,5},{7,6},{8,7},{9,8},{10,9},{11,1... | collective-permute-start | bytes 786440 | tf_op jit(solution)/shard_map/while/body/eval_jaxpr/ppermute | solution.py:25
  226.5 3.1 copy-start.1
  236.7 8.2 %collective-permute-start.1 = (bf16[1,1,16,16,512]{4,3,2,1,0:T(8,128)(2,1)S(1)}, bf16[1,1,16,16,512]{4,3,2,1,0:T(8,128)(2,1)S(1)}, u32[]{:S(2)}, u32[]{:S(2)}) collective-permute-start(bf16[1,1,16,16,512]{4,3,2,1,0:T(8,128)(2,1)S(1)} %broadcast_select_fusion.3), channel_id=1, source_target_pairs={{0,16},{1,17},{2,18},{3,19},{4,20},{5,21},{6,22},{7,23},{8,24},{9,... | collective-permute-start | bytes 786440 | tf_op jit(solution)/shard_map/while/body/eval_jaxpr/ppermute | solution.py:12
  241.0 7.5 %collective-permute-start = (bf16[1,16,16,512]{3,2,1,0:T(8,128)(2,1)}, bf16[1,16,16,512]{3,2,1,0:T(8,128)(2,1)S(1)}, u32[]{:S(2)}, u32[]{:S(2)}) collective-permute-start(bf16[1,16,16,512]{3,2,1,0:T(8,128)(2,1)} %get-tuple-element.384), channel_id=1, source_target_pairs={{0,16},{1,17},{2,18},{3,19},{4,20},{5,21},{6,22},{7,23},{8,24},{9,... | collective-permute-start | bytes 786440 | tf_op jit(solution)/shard_map/while/body/eval_jaxpr/ppermute | solution.py:12
  248.6 18.7 %copy-start.2 = (bf16[3,512,512]{2,1,0:T(8,128)(2,1)S(1)}, bf16[3,512,512]{2,1,0:T(8,128)(2,1)}, u32[]{:S(2)}) copy-start(bf16[3,512,512]{2,1,0:T(8,128)(2,1)} %get-tuple-element.414) | copy-start | bytes 4718596 | tf_op jit(solution)/shard_map/while
  250.5 3.1 copy-start
  256.0 8.2 %collective-permute-start.2 = (bf16[1,16,16,512]{3,2,1,0:T(8,128)(2,1)S(1)}, bf16[1,16,16,512]{3,2,1,0:T(8,128)(2,1)S(1)}, u32[]{:S(2)}, u32[]{:S(2)}) collective-permute-start(bf16[1,16,16,512]{3,2,1,0:T(8,128)(2,1)S(1)} %get-tuple-element.419), channel_id=1, source_target_pairs={{0,1},{1,2},{2,3},{3,4},{4,5},{5,6},{6,7},{7,8},{8,9},{9,10},{10,1... | collective-permute-start | bytes 786440 | tf_op jit(solution)/shard_map/while/body/eval_jaxpr/ppermute | solution.py:23
  262.9 4.4 %collective-permute-start.3 = (bf16[1,16,16,512]{3,2,1,0:T(8,128)(2,1)S(1)}, bf16[1,16,16,512]{3,2,1,0:T(8,128)(2,1)}, u32[]{:S(2)}, u32[]{:S(2)}) collective-permute-start(bf16[1,16,16,512]{3,2,1,0:T(8,128)(2,1)S(1)} %get-tuple-element.419), channel_id=1, source_target_pairs={{1,0},{2,1},{3,2},{4,3},{5,4},{6,5},{7,6},{8,7},{9,8},{10,9},{11,1... | collective-permute-start | bytes 786440 | tf_op jit(solution)/shard_map/while/body/eval_jaxpr/ppermute | solution.py:25
  267.3 3.1 copy-start.1
  277.5 8.2 %collective-permute-start.1 = (bf16[1,1,16,16,512]{4,3,2,1,0:T(8,128)(2,1)S(1)}, bf16[1,1,16,16,512]{4,3,2,1,0:T(8,128)(2,1)S(1)}, u32[]{:S(2)}, u32[]{:S(2)}) collective-permute-start(bf16[1,1,16,16,512]{4,3,2,1,0:T(8,128)(2,1)S(1)} %broadcast_select_fusion.3), channel_id=1, source_target_pairs={{0,16},{1,17},{2,18},{3,19},{4,20},{5,21},{6,22},{7,23},{8,24},{9,... | collective-permute-start | bytes 786440 | tf_op jit(solution)/shard_map/while/body/eval_jaxpr/ppermute | solution.py:12
  281.9 6.8 %collective-permute-start = (bf16[1,16,16,512]{3,2,1,0:T(8,128)(2,1)}, bf16[1,16,16,512]{3,2,1,0:T(8,128)(2,1)S(1)}, u32[]{:S(2)}, u32[]{:S(2)}) collective-permute-start(bf16[1,16,16,512]{3,2,1,0:T(8,128)(2,1)} %get-tuple-element.384), channel_id=1, source_target_pairs={{0,16},{1,17},{2,18},{3,19},{4,20},{5,21},{6,22},{7,23},{8,24},{9,... | collective-permute-start | bytes 786440 | tf_op jit(solution)/shard_map/while/body/eval_jaxpr/ppermute | solution.py:12
  288.6 23.3 %copy-start.2 = (bf16[3,512,512]{2,1,0:T(8,128)(2,1)S(1)}, bf16[3,512,512]{2,1,0:T(8,128)(2,1)}, u32[]{:S(2)}) copy-start(bf16[3,512,512]{2,1,0:T(8,128)(2,1)} %get-tuple-element.414) | copy-start | bytes 4718596 | tf_op jit(solution)/shard_map/while
  290.6 3.1 copy-start
  296.0 9.9 %collective-permute-start.2 = (bf16[1,16,16,512]{3,2,1,0:T(8,128)(2,1)S(1)}, bf16[1,16,16,512]{3,2,1,0:T(8,128)(2,1)S(1)}, u32[]{:S(2)}, u32[]{:S(2)}) collective-permute-start(bf16[1,16,16,512]{3,2,1,0:T(8,128)(2,1)S(1)} %get-tuple-element.419), channel_id=1, source_target_pairs={{0,1},{1,2},{2,3},{3,4},{4,5},{5,6},{6,7},{7,8},{8,9},{9,10},{10,1... | collective-permute-start | bytes 786440 | tf_op jit(solution)/shard_map/while/body/eval_jaxpr/ppermute | solution.py:23
  304.6 7.4 %collective-permute-start.3 = (bf16[1,16,16,512]{3,2,1,0:T(8,128)(2,1)S(1)}, bf16[1,16,16,512]{3,2,1,0:T(8,128)(2,1)}, u32[]{:S(2)}, u32[]{:S(2)}) collective-permute-start(bf16[1,16,16,512]{3,2,1,0:T(8,128)(2,1)S(1)} %get-tuple-element.419), channel_id=1, source_target_pairs={{1,0},{2,1},{3,2},{4,3},{5,4},{6,5},{7,6},{8,7},{9,8},{10,9},{11,1... | collective-permute-start | bytes 786440 | tf_op jit(solution)/shard_map/while/body/eval_jaxpr/ppermute | solution.py:25
  312.0 3.1 copy-start.1
  322.2 8.2 %collective-permute-start.1 = (bf16[1,1,16,16,512]{4,3,2,1,0:T(8,128)(2,1)S(1)}, bf16[1,1,16,16,512]{4,3,2,1,0:T(8,128)(2,1)S(1)}, u32[]{:S(2)}, u32[]{:S(2)}) collective-permute-start(bf16[1,1,16,16,512]{4,3,2,1,0:T(8,128)(2,1)S(1)} %broadcast_select_fusion.3), channel_id=1, source_target_pairs={{0,16},{1,17},{2,18},{3,19},{4,20},{5,21},{6,22},{7,23},{8,24},{9,... | collective-permute-start | bytes 786440 | tf_op jit(solution)/shard_map/while/body/eval_jaxpr/ppermute | solution.py:12
  326.5 6.8 %collective-permute-start = (bf16[1,16,16,512]{3,2,1,0:T(8,128)(2,1)}, bf16[1,16,16,512]{3,2,1,0:T(8,128)(2,1)S(1)}, u32[]{:S(2)}, u32[]{:S(2)}) collective-permute-start(bf16[1,16,16,512]{3,2,1,0:T(8,128)(2,1)} %get-tuple-element.384), channel_id=1, source_target_pairs={{0,16},{1,17},{2,18},{3,19},{4,20},{5,21},{6,22},{7,23},{8,24},{9,... | collective-permute-start | bytes 786440 | tf_op jit(solution)/shard_map/while/body/eval_jaxpr/ppermute | solution.py:12
  333.3 17.9 %copy-start.2 = (bf16[3,512,512]{2,1,0:T(8,128)(2,1)S(1)}, bf16[3,512,512]{2,1,0:T(8,128)(2,1)}, u32[]{:S(2)}) copy-start(bf16[3,512,512]{2,1,0:T(8,128)(2,1)} %get-tuple-element.414) | copy-start | bytes 4718596 | tf_op jit(solution)/shard_map/while
  335.3 9.9 %collective-permute-start.2 = (bf16[1,16,16,512]{3,2,1,0:T(8,128)(2,1)S(1)}, bf16[1,16,16,512]{3,2,1,0:T(8,128)(2,1)S(1)}, u32[]{:S(2)}, u32[]{:S(2)}) collective-permute-start(bf16[1,16,16,512]{3,2,1,0:T(8,128)(2,1)S(1)} %get-tuple-element.419), channel_id=1, source_target_pairs={{0,1},{1,2},{2,3},{3,4},{4,5},{5,6},{6,7},{7,8},{8,9},{9,10},{10,1... | collective-permute-start | bytes 786440 | tf_op jit(solution)/shard_map/while/body/eval_jaxpr/ppermute | solution.py:23
  343.9 7.4 %collective-permute-start.3 = (bf16[1,16,16,512]{3,2,1,0:T(8,128)(2,1)S(1)}, bf16[1,16,16,512]{3,2,1,0:T(8,128)(2,1)}, u32[]{:S(2)}, u32[]{:S(2)}) collective-permute-start(bf16[1,16,16,512]{3,2,1,0:T(8,128)(2,1)S(1)} %get-tuple-element.419), channel_id=1, source_target_pairs={{1,0},{2,1},{3,2},{4,3},{5,4},{6,5},{7,6},{8,7},{9,8},{10,9},{11,1... | collective-permute-start | bytes 786440 | tf_op jit(solution)/shard_map/while/body/eval_jaxpr/ppermute | solution.py:25
Sparse Core Ops, SparseCore 0:
  9.6 55.8 all-gather.8
  67.7 38.1 all-gather.6
  108.1 51.6 all-gather.4
  354.5 65.8 all-reduce.3
